TPU v7x, 256 devices: a whole 4x4x8 slice. The times are simulated.
256 devices in a mesh: across: 4 (over x), along: 8 (over z), gas: 8 (over y, core).
Axes of the slice: x: 4, y: 4, z: 8, core: 2. Of those that a mesh axis runs over, the one named last changes fastest.
Arguments:
- gas_vel: float32 [2, 2048, 1024], P(None, ('along', 'gas'), 'across'), may hold values from -0.5 to 1.5
- viscosity: float32 [2048, 1024], P(('along', 'gas'), 'across'), may hold values from 0.05 to 0.5
- positions: float32 [2, 128, 64, 128], P(None, 'along', ('across', 'gas')), may hold values from 0 to 1
- velocities: float32 [2, 128, 64, 128], P(None, 'along', ('across', 'gas')), may hold values from -4 to 4
- radius: float32 [128, 64, 128], P('along', ('across', 'gas')), may hold values from 0.5 to 0.9
- drag_coef: float32 [128, 64, 128], P('along', ('across', 'gas')), may hold values from 0.5 to 4
- counts: int32 [128, 64], P('along', ('across', 'gas')), may hold values from 16 to 128
- pattern: int32 [128, 64, 9], P('along', ('across', 'gas')), may hold values 0 or 1
- cell_index: int32 [128, 64, 128], P('along', ('across', 'gas')), may hold values from 0 to 238, as said below
- cell_frac: int32 [2, 128, 64, 128], P(None, 'along', ('across', 'gas')), may hold values from 0 to 1024
Outputs:
- particles_out: float32 [4, 128, 64, 128], P(None, 'along', ('across', 'gas'))
- gas_out: float32 [2, 2048, 1024], P(None, ('along', 'gas'), 'across')
Inputs may be any that keep to these rules, and one draw needn't show every extreme that they name: `cell_index`: row*16 + col with row and col each from 0 to 14.
All inputs are finite; a program needn't handle non-finite values. Where the computation divides by a largest or mean magnitude, that divisor is 1e-20 or more. No bound on the sum of `pattern` on one device may be relied on, other than what follows from the above.
Results may differ from a plain program's by a relative error of at most 0.0003.
Values sent between devices are 32-bit elements; how exact they have to be, the bound alone decides.
A program may use at most 64 MiB of HBM per device.

v0:
```python
import functools

import jax
import jax.numpy as jnp
from jax import lax
from jax.experimental import pallas as pl
from jax.experimental.pallas import tpu as pltpu
from jax.sharding import PartitionSpec as P

ALONG_GAS = ("along", "gas")
ACROSS_GAS = ("across", "gas")
MESH_ID = pl.DeviceIdType.MESH
OFFSETS = [(-1, -1), (-1, 0), (-1, 1), (0, -1), (0, 0), (0, 1), (1, -1), (1, 0), (1, 1)]
DEAD = -16384.0
F32 = jnp.float32
BF16 = jnp.bfloat16
STRIDE = 136
BLOCK, BLOCK_BITS = 64, 6
EMPTY = 1344
REACH = 2.4
MOVE_LIMIT = int((REACH - 1.9) * 4096)
VMEM_SPEC = pl.BlockSpec(memory_space=pltpu.VMEM)
SMEM_SPEC = pl.BlockSpec(memory_space=pltpu.SMEM)
N_ACROSS, N_ALONG, N_GAS = 4, 8, 8


def iota(shape, dim):
    return lax.broadcasted_iota(jnp.int32, shape, dim)


def ext_row(ii, jj):
    base = {-1: 32, 0: 0, 1: 16, 2: 48}[jj]
    return jnp.where(ii < 0, 64 + 8 * (jj + 1) + 7, jnp.where(ii > 15, 96 + 8 * (jj + 1), base + ii))


def by_column(ref, *lead):
    return jnp.concatenate([ref[(*lead, pl.ds(0, 16, stride=2), slice(None))],
                            ref[(*lead, pl.ds(1, 16, stride=2), slice(None))]], axis=0)


def prepare_state(st, pos, vel, rad, counts):
    row32 = iota((32, 128), 0)
    slot = iota((32, 128), 1)
    cnt = jnp.zeros((32, 128), jnp.int32)
    for j in range(2):
        for i in range(16):
            cnt = jnp.where(row32 == j * 16 + i, counts[j, i], cnt)
    alive = slot < cnt
    z, x = by_column(pos, 0) * 16.0, by_column(pos, 1) * 16.0
    st[0, 0:32, :], st[1, 0:32, :] = z, x
    st[2, 0:32, :], st[3, 0:32, :] = by_column(vel, 0), by_column(vel, 1)
    st[4, 0:32, :] = jnp.where(alive, by_column(rad), DEAD)
    low_x, high_x = x < REACH, x > 16.0 - REACH

    def three(low, mid, high):
        return jnp.where(low_x, low, jnp.where(high_x, high, mid))

    kind = jnp.where(z < REACH, three(0, 1, 2), jnp.where(z > 16.0 - REACH, three(6, 5, 4), three(7, 8, 3)))
    kind = jnp.where(alive, kind, 9)
    member = jnp.concatenate([jnp.where(kind == c, 1.0, 0.0) for c in range(9)], axis=0).astype(BF16)
    before = jnp.where((iota((128, 256), 0) < iota((128, 256), 1)) | (iota((128, 256), 1) >= 128), 1.0, 0.0)
    ranks = jnp.dot(member, before.astype(BF16), preferred_element_type=F32)
    rank = jnp.full((32, 128), -1.0, F32)
    start = [jnp.zeros((32, 128), F32)]
    for c in range(9):
        here = ranks[c * 32:(c + 1) * 32]
        rank = jnp.where(kind == c, start[c] + here[:, 0:128], rank)
        start.append(start[c] + here[:, 128:256])
    st[5, 0:32, :] = rank
    start = [v.astype(jnp.int32) for v in start]
    wrap = ((start[1] + 7) & -8) > start[6]
    zero = jnp.zeros((32, 128), jnp.int32)
    windows = [(start[4], start[5]), (start[4], start[7]), (start[6], start[7]), (start[2], start[5]),
               (zero, start[9]), (jnp.where(wrap, 0, start[6]), start[8]), (start[2], start[3]),
               (zero, start[3]), (zero, start[1]), (zero, jnp.where(wrap, 0, start[1]))]
    table = zero
    for w, (low, high) in enumerate(windows):
        table = jnp.where(slot == 2 * w, low, jnp.where(slot == 2 * w + 1, (high - low + 7) & -8, table))
    st[6, 0:32, :] = table.astype(F32)


def prep_kernel(gas, visc, pos, vel, rad, counts, st, gp, mx):
    rate = jnp.abs(gas[0]) + jnp.abs(gas[1]) + 4.0 * visc[...]
    top = jnp.max(jnp.max(rate, axis=1, keepdims=True), axis=0, keepdims=True)
    mx[...] = jnp.broadcast_to(top, (8, 128))
    lane = iota((16, 128), 1)
    for g in range(N_GAS):
        blk = slice((g // 4) * 128, (g // 4) * 128 + 128)
        off = (g % 4) * 32
        for k in range(2):
            low = gas[k, 0:16, blk]
            high = gas[k, 16:32, blk]
            low = pltpu.roll(low, (128 - off) % 128, 1) if off else low
            shift = (160 - off) % 128
            high = pltpu.roll(high, shift, 1) if shift else high
            piece = jnp.where(lane < 32, low, jnp.where(lane < 64, high, 0.0))
            gp[g, k * 16:(k + 1) * 16, :] = piece
    prepare_state(st, pos, vel, rad, counts)
    st[7] = jnp.zeros((32, 128), F32)


def comm_kernel(first, *refs):
    if first:
        (st, pc, mx, gas, ext, pv, red, gr, gc, mb, m1, m2,
         own_sem, hs, hr, ps, pr, rs, rr, es, er) = refs
    else:
        (st, pc, mx, ext, pv, red, mb, m1, m2,
         own_sem, hs, hr, ps, pr, rs, rr) = refs
    ax, al, g = lax.axis_index("across"), lax.axis_index("along"), lax.axis_index("gas")
    up, down = lax.rem(al + 1, N_ALONG), lax.rem(al + N_ALONG - 1, N_ALONG)
    lin = ax * N_GAS + g
    has_left, has_right = lin > 0, lin < N_ACROSS * N_GAS - 1
    left = jnp.maximum(lin - 1, 0)
    right = jnp.minimum(lin + 1, N_ACROSS * N_GAS - 1)

    def col(index, along):
        return {"across": lax.div(index, N_GAS), "along": along, "gas": lax.rem(index, N_GAS)}

    slab = al * N_GAS + g
    slabs = N_ALONG * N_GAS
    after, before = lax.rem(slab + 1, slabs), lax.rem(slab + slabs - 1, slabs)

    def slab_id(index):
        return {"across": ax, "along": lax.div(index, N_GAS), "gas": lax.rem(index, N_GAS)}

    barrier = pltpu.get_barrier_semaphore()

    def greet(device):
        pl.semaphore_signal(barrier, inc=1, device_id=device, device_id_type=MESH_ID)

    for k in range(1, N_ACROSS):
        greet({"across": lax.rem(ax + k, N_ACROSS)})
    for k in range(1, N_GAS):
        greet({"gas": lax.rem(g + k, N_GAS)})
    for k in range(1, N_ALONG):
        greet({"along": lax.rem(al + k, N_ALONG)})
    expect = N_ACROSS + N_GAS + N_ALONG - 3
    if first:
        greet(slab_id(after))
        greet(slab_id(before))
        expect += 2

    @pl.when(has_left)
    def _():
        for along in (down, al, up):
            greet(col(left, along))

    @pl.when(has_right)
    def _():
        for along in (down, al, up):
            greet(col(right, along))

    own = pltpu.make_async_copy(st, ext.at[:, pl.ds(0, 32)], own_sem.at[0])
    own.start()
    own_piece = pltpu.make_async_copy(pc.at[g], pv.at[g], own_sem.at[1])
    own_piece.start()

    @pl.when(jnp.logical_not(has_left))
    def _():
        ext[:, 32:48, :] = jnp.zeros((8, 16, 128), F32)
        ext[:, 64:72, :] = jnp.zeros((8, 8, 128), F32)
        ext[:, 96:104, :] = jnp.zeros((8, 8, 128), F32)

    @pl.when(jnp.logical_not(has_right))
    def _():
        ext[:, 48:64, :] = jnp.zeros((8, 16, 128), F32)
        ext[:, 88:96, :] = jnp.zeros((8, 8, 128), F32)
        ext[:, 120:128, :] = jnp.zeros((8, 8, 128), F32)

    if first:
        @pl.when(ax == 0)
        def _():
            gc[0] = jnp.zeros((2, 32, 128), F32)

        @pl.when(ax == N_ACROSS - 1)
        def _():
            gc[1] = jnp.zeros((2, 32, 128), F32)

    sides = jnp.where(has_left, 3, 0) + jnp.where(has_right, 3, 0)
    pl.semaphore_wait(barrier, expect + sides)

    def remote(src, dst, send, recv, device):
        return pltpu.make_async_remote_copy(
            src_ref=src, dst_ref=dst, send_sem=send, recv_sem=recv,
            device_id=device, device_id_type=MESH_ID,
        )

    def reduce_sends(phase, src, axis, me, size):
        out = []
        for k in range(1, size):
            out.append(remote(src, mb.at[phase, me], rs.at[phase, k], rr.at[phase, k],
                              {axis: lax.rem(me + k, size)}))
        for c in out:
            c.start()
        return out

    phase0 = reduce_sends(0, mx, "across", ax, N_ACROSS)

    def halo(c, src_rows, size, dst_row, device):
        return remote(st.at[pl.ds(0, 7), pl.ds(src_rows, size)],
                      ext.at[pl.ds(0, 7), pl.ds(dst_row, size)], hs.at[c], hr.at[c], device)

    lefts = [halo(0, 0, 16, 48, col(left, al)),
             halo(1, 8, 8, 64 + 24, col(left, up)),
             halo(2, 0, 8, 96 + 24, col(left, down))]
    rights = [halo(3, 16, 16, 32, col(right, al)),
              halo(4, 24, 8, 64, col(right, up)),
              halo(5, 16, 8, 96, col(right, down))]
    rows = [halo(6, 8, 8, 64 + 8, {"along": up}),
            halo(7, 24, 8, 64 + 16, {"along": up}),
            halo(8, 0, 8, 96 + 8, {"along": down}),
            halo(9, 16, 8, 96 + 16, {"along": down})]

    @pl.when(has_left)
    def _():
        for c in lefts:
            c.start()

    @pl.when(has_right)
    def _():
        for c in rights:
            c.start()

    for c in rows:
        c.start()
    pieces = []
    for k in range(1, N_GAS):
        peer = lax.rem(g + k, N_GAS)
        c = remote(pc.at[peer], pv.at[g], ps.at[k], pr.at[k], {"gas": peer})
        c.start()
        pieces.append(c)
    if first:
        edges = [remote(gas.at[:, pl.ds(24, 8)], gr.at[0], es.at[0], er.at[0], slab_id(after)),
                 remote(gas.at[:, pl.ds(0, 8)], gr.at[1], es.at[1], er.at[1], slab_id(before))]
        for c in edges:
            c.start()
        to_right = remote(gas.at[:, :, pl.ds(128, 128)], gc.at[0], es.at[2], er.at[2],
                          {"across": jnp.minimum(ax + 1, N_ACROSS - 1)})
        to_left = remote(gas.at[:, :, pl.ds(0, 128)], gc.at[1], es.at[3], er.at[3],
                         {"across": jnp.maximum(ax - 1, 0)})

        @pl.when(ax < N_ACROSS - 1)
        def _():
            to_right.start()

        @pl.when(ax > 0)
        def _():
            to_left.start()

    def combine(phase, mine, me, size, copies):
        for c in copies:
            c.wait_recv()
        mb[phase, me] = mine
        total = mb[phase, 0]
        for k in range(1, size):
            total = jnp.maximum(total, mb[phase, k]) if first else total + mb[phase, k]
        return total

    m1[...] = combine(0, mx[...], ax, N_ACROSS, phase0)
    phase1 = reduce_sends(1, m1, "gas", g, N_GAS)
    m2[...] = combine(1, m1[...], g, N_GAS, phase1)
    phase2 = reduce_sends(2, m2, "along", al, N_ALONG)
    red[...] = combine(2, m2[...], al, N_ALONG, phase2)

    own.wait()
    own_piece.wait()
    for c in phase0 + phase1 + phase2:
        c.wait_send()
    for c in rows + pieces:
        c.wait()

    @pl.when(has_left)
    def _():
        for c in lefts:
            c.wait_send()
        for c in rights:
            c.wait_recv()

    @pl.when(has_right)
    def _():
        for c in rights:
            c.wait_send()
        for c in lefts:
            c.wait_recv()

    if first:
        for c in edges:
            c.wait()

        @pl.when(ax < N_ACROSS - 1)
        def _():
            to_right.wait_send()
            to_left.wait_recv()

        @pl.when(ax > 0)
        def _():
            to_left.wait_send()
            to_right.wait_recv()


def exchange(first, st, pc, mx, gas=None):
    out_shape = [jax.ShapeDtypeStruct((8, 128, 128), F32),
                 jax.ShapeDtypeStruct((8, 32, 128), F32),
                 jax.ShapeDtypeStruct((8, 128), F32)]
    scratch = [pltpu.VMEM((3, 8, 8, 128), F32), pltpu.VMEM((8, 128), F32), pltpu.VMEM((8, 128), F32),
               pltpu.SemaphoreType.DMA((2,)),
               pltpu.SemaphoreType.DMA((10,)), pltpu.SemaphoreType.DMA((10,)),
               pltpu.SemaphoreType.DMA((8,)), pltpu.SemaphoreType.DMA((8,)),
               pltpu.SemaphoreType.DMA((3, 8)), pltpu.SemaphoreType.DMA((3, 8))]
    args = [st, pc, mx]
    if first:
        args.append(gas)
        out_shape += [jax.ShapeDtypeStruct((2, 2, 8, 256), F32), jax.ShapeDtypeStruct((2, 2, 32, 128), F32)]
        scratch += [pltpu.SemaphoreType.DMA((4,)), pltpu.SemaphoreType.DMA((4,))]
    return pl.pallas_call(
        functools.partial(comm_kernel, first),
        out_shape=out_shape,
        in_specs=[VMEM_SPEC] * len(args),
        out_specs=[VMEM_SPEC] * len(out_shape),
        scratch_shapes=scratch,
        compiler_params=pltpu.CompilerParams(collective_id=0 if first else 1, has_side_effects=True),
        name="exchange_first" if first else "exchange_second",
    )(*args)


def split3(x):
    hi = x.astype(BF16).astype(F32)
    rest = x - hi
    mid = rest.astype(BF16).astype(F32)
    return hi, mid, rest - mid


def contact_forces(ext, pat, meta, ints, qt, lst, rhs, frc, sem):
    ints[...] = ext[6 * 128:7 * 128, :].astype(jnp.int32)
    to_smem = pltpu.make_async_copy(ints, meta, sem)
    to_smem.start()
    slot = iota((128, 128), 0).astype(F32)
    attr_row = iota((8, 128), 0)
    zero8 = jnp.zeros((8, 128), F32)
    tail = jnp.concatenate([zero8, jnp.ones((24, 128), F32), zero8], axis=0)

    def parts(row):
        block = ext[pl.ds(row, 8, stride=128), :]
        return split3(jnp.where(attr_row < 5, block, 0.0))

    def transposed(row):
        hi, mid, lo = parts(row)
        rows = jnp.concatenate([hi, mid, lo, tail], axis=0).astype(BF16)
        place = (slot == ext[pl.ds(row + 5 * 128, 1), :]).astype(F32).astype(BF16)
        turned = lax.dot_general(place, rows, (((1,), (1,)), ((), ())), preferred_element_type=F32)
        start = row * STRIDE if isinstance(row, int) else pl.multiple_of(row * STRIDE, 8)
        qt[pl.ds(start, 128), 0:64] = turned
        start = start + 128 if isinstance(row, int) else pl.multiple_of(start + 128, 8)
        qt[pl.ds(start, 8), :] = zero8

    def some(step, carry):
        for u in range(4):
            transposed(step * 4 + u)
        return carry

    lax.fori_loop(0, 16, some, 0)
    for c in range(4):
        transposed(64 + 8 * c + 7)
        transposed(96 + 8 * c)

    block_of = iota((32, 640), 1) >> 7
    row_of = iota((32, 640), 0)
    attr_of = row_of & 7
    own_scale = jnp.where(block_of < 2, -1.0, jnp.where(block_of < 4, 2.0, 1.0))
    const = jnp.where((attr_of == block_of) & (row_of < 24), own_scale, 0.0)
    const = jnp.where((row_of == 24) & (block_of == 0) | (row_of == 25) & (block_of == 1), -16.0, const)
    for u in range(2):
        rhs[u, 0:32, :] = const.astype(BF16)
        lst[u, EMPTY:EMPTY + BLOCK, :] = jnp.zeros((BLOCK, 128), F32)
    to_smem.wait()
    lane = iota((8, 128), 1)

    def row_step(i, carry):
        blocks = []
        for j in range(2):
            work = lst.at[j]
            mine = j * 16 + i
            hi, mid, lo = parts(mine)
            columns = []
            for a in range(5):
                keep = attr_row == a
                scale = 1.0 if a in (0, 1, 4) else -2.0
                columns.append(jnp.concatenate(
                    [jnp.where(keep, hi * scale, 0.0), jnp.where(keep, mid * scale, 0.0),
                     jnp.where(keep, lo * scale, 0.0), zero8], axis=0))
            rhs[j, 32:64, :] = jnp.concatenate(columns, axis=1).astype(BF16)
            moved = meta[mine, 20]
            off = i * 0
            over = i * 0
            windows = []
            for w in (4, 0, 1, 2, 3, 5, 6, 7, 8, 9):
                di, dj = OFFSETS[5 if w == 9 else w]
                row = ext_row(i + di, j + dj)
                first, size = meta[row, 2 * w], meta[row, 2 * w + 1]
                if w != 4:
                    near = moved + meta[row, 20] <= MOVE_LIMIT
                    first = jnp.where(near, first, 0)
                    size = jnp.where(near, size, 0 if w == 9 else meta[row, 9])
                size = size * pat[5 if w == 9 else w, j, i]
                mark = jnp.where(lane == 24, float(di), jnp.where(lane == 25, float(dj), 0.0))
                start = row * STRIDE + first
                chunks = 16 if w == 4 else 4 if w in (1, 3, 5, 7) else 1
                for c in range(chunks):
                    work[pl.ds(pl.multiple_of(off + c * 8, 8), 8), :] = qt[pl.ds(start + c * 8, 8), :] + mark
                windows.append((start, size, mark))
                off = off + size
                over = jnp.maximum(over, size - chunks * 8)

            @pl.when(over > 0)
            def _():
                to = i * 0
                for start, size, mark in windows:
                    def copy(c, carry, start=start, mark=mark, to=to):
                        work[pl.ds(pl.multiple_of(to + c * 8, 8), 8), :] = qt[pl.ds(start + c * 8, 8), :] + mark
                        return carry
                    lax.fori_loop(0, size >> 3, copy, 0)
                    to = to + size

            for c in range(BLOCK // 8):
                work[pl.ds(pl.multiple_of(off + c * 8, 8), 8), :] = zero8
            blocks.append((off + BLOCK - 1) >> BLOCK_BITS)
        right = [rhs[0], rhs[1]]

        def block(b, acc):
            out = []
            for j in range(2):
                at = jnp.where(b < blocks[j], b * BLOCK, EMPTY)
                q = lst[j, pl.ds(pl.multiple_of(at, 8), BLOCK), 0:64].astype(BF16)
                got = jnp.dot(q, right[j], preferred_element_type=F32)
                rz, rx = got[:, 0:128], got[:, 128:256]
                dz, dx = got[:, 256:384], got[:, 384:512]
                d2 = rz * rz + rx * rx + 0.0001
                inv = lax.rsqrt(d2)
                depth = jnp.maximum(got[:, 512:640] - d2 * inv, 0.0)
                push = depth * inv * (40.0 + (dz * rz + dx * rx) * inv)
                out.append(acc[2 * j] + jnp.sum((push * rz).reshape(BLOCK // 8, 8, 128), axis=0))
                out.append(acc[2 * j + 1] + jnp.sum((push * rx).reshape(BLOCK // 8, 8, 128), axis=0))
            return tuple(out)

        acc = lax.fori_loop(0, jnp.maximum(blocks[0], blocks[1]), block, (zero8,) * 4)
        for j in range(2):
            for k in range(2):
                frc[pl.ds(pl.multiple_of(((k * 2 + j) * 16 + i) * 8, 8), 8), :] = acc[2 * j + k]
        return carry

    lax.fori_loop(0, 16, row_step, 0)
    return [sum(frc[pl.ds(k * 256 + r, 32, stride=8), :] for r in range(8)) for k in range(2)]


def first_kernel(ext, gv, rate, idx, frac, coef, pat, st2, dp, tot, dr2, inv_out,
                 meta, ints, qt, lst, rhs, frc, itp, sem):
    def weights(r, t4):
        index = idx[pl.ds(r, 1), :]
        row, column = index >> 4, index & 15
        share_z = frac[0, pl.ds(r, 1), :].astype(F32) / 1024.0
        share_x = frac[1, pl.ds(r, 1), :].astype(F32) / 1024.0
        c64 = iota((64, 128), 0) - t4 * 16
        wx = jnp.where(c64 == column, 1.0 - share_x, jnp.where(c64 == column + 1, share_x, 0.0))
        r16 = iota((16, 128), 0)
        wz = jnp.where(r16 == row, 1.0 - share_z, jnp.where(r16 == row + 1, share_z, 0.0))
        return wz, wx

    def sample(h, carry):
        field = gv[h][:, 0:64]
        for t in range(2):
            for j in range(2):
                wz, wx = weights(4 * h + 2 * t + j, t * 2 + j)
                along = jnp.dot(field, wx, precision=lax.Precision.HIGHEST, preferred_element_type=F32)
                for k in range(2):
                    itp[k, pl.ds(j * 16 + 2 * h + t, 1), :] = jnp.sum(
                        wz * along[k * 16:(k + 1) * 16], axis=0, keepdims=True)
        return carry

    lax.fori_loop(0, 8, sample, 0)
    force = contact_forces(ext, pat, meta, ints, qt, lst, rhs, frc, sem)
    step = 0.2 / rate[0:1, :]
    drag = by_column(coef)
    radius = ext[4 * 128:4 * 128 + 32, :]
    alive = jnp.where(radius > 0.0, 1.0, 0.0)
    inverse = jnp.where(radius > 0.0, 0.36 / (radius * radius), 0.0)
    inv_out[...] = inverse
    means = []
    moved = jnp.zeros((32, 128), F32)
    for k in range(2):
        place = ext[k * 128:k * 128 + 32, :]
        speed = ext[(2 + k) * 128:(2 + k) * 128 + 32, :]
        drag1 = drag * (itp[k] - speed)
        speed2 = speed + step * (inverse * (force[k] + drag1) - (alive if k == 0 else 0.0))
        st2[k] = place + step * speed2
        moved = jnp.maximum(moved, alive * jnp.abs(step * speed2))
        st2[2 + k] = speed2
        drag2 = drag * (itp[k] - speed2)
        dr2[k] = drag2
        mean = 0.5 * (alive * drag1 + alive * drag2)
        itp[k] = mean
        means.append(jnp.sum(jnp.sum(mean, axis=1, keepdims=True), axis=0, keepdims=True))
    st2[4] = radius
    st2[5] = ext[5 * 128:5 * 128 + 32, :]
    far = jnp.max(moved, axis=1, keepdims=True)
    far = jnp.where(far < 100.0, far, 100.0) * 4096.0 + 1.0
    st2[6] = jnp.where(iota((32, 128), 1) == 20, far, ext[6 * 128:6 * 128 + 32, :])
    st2[7] = jnp.zeros((32, 128), F32)
    tot[...] = jnp.where(iota((8, 128), 0) == 0, means[0], means[1])

    def spread(h, carry):
        total = jnp.zeros((32, 64), F32)
        for t in range(2):
            for j in range(2):
                wz, wx = weights(4 * h + 2 * t + j, t * 2 + j)
                m0 = itp[0, pl.ds(j * 16 + 2 * h + t, 1), :]
                m1 = itp[1, pl.ds(j * 16 + 2 * h + t, 1), :]
                lhs = jnp.concatenate([wz * m0, wz * m1], axis=0)
                total = total + lax.dot_general(lhs, wx, (((1,), (1,)), ((), ())),
                                                precision=lax.Precision.HIGHEST, preferred_element_type=F32)
        dp[h, :, 0:64] = total
        dp[h, :, 64:128] = jnp.zeros((32, 64), F32)
        return carry

    lax.fori_loop(0, 8, spread, 0)


def gas_step_update(gas, visc, gr, gc, dv, tot, rate, out):
    gas_step = 0.4 / rate[0:1, 0:1]
    lane = iota((32, 256), 1)
    row = iota((32, 256), 0)
    lane16 = iota((16, 128), 1) >> 5
    for k in range(2):
        u = gas[k]
        upper = jnp.where(row == 31, gr[1, k, 0:1, :], pltpu.roll(u, 31, 0))
        lower = jnp.where(row == 0, gr[0, k, 7:8, :], pltpu.roll(u, 1, 0))
        right = jnp.where(lane == 255, gc[1, k, :, 0:1], pltpu.roll(u, 255, 1))
        left = jnp.where(lane == 0, gc[0, k, :, 127:128], pltpu.roll(u, 1, 1))
        laplace = upper + lower + right + left - 4.0 * u
        advect = gas[0] * (upper - lower) * 0.5 + gas[1] * (right - left) * 0.5
        quads = []
        for t in range(2):
            halves = []
            for b in range(2):
                whole = None
                for q in range(4):
                    piece = dv[4 * b + q, k * 16:(k + 1) * 16, :]
                    shift = (q * 32 - t * 32) % 128
                    piece = pltpu.roll(piece, shift, 1) if shift else piece
                    whole = piece if whole is None else jnp.where(lane16 == q, piece, whole)
                halves.append(whole)
            quads.append(jnp.concatenate(halves, axis=1))
        deposit = jnp.concatenate(quads, axis=0)
        source = tot[k:k + 1, 0:1] / 2097152.0 - deposit
        out[k] = u + gas_step * (visc[...] * laplace - advect + source)


def second_kernel(ext, dv, tot, rate, dr2, inverse, gas, visc, gr, gc, pat, part, out,
                  meta, ints, qt, lst, rhs, frc, sem):
    force = contact_forces(ext, pat, meta, ints, qt, lst, rhs, frc, sem)
    step = 0.2 / rate[0:1, :]
    radius = ext[4 * 128:4 * 128 + 32, :]
    alive = jnp.where(radius > 0.0, 1.0, 0.0)
    for k in range(2):
        place = ext[k * 128:k * 128 + 32, :]
        speed = ext[(2 + k) * 128:(2 + k) * 128 + 32, :]
        speed2 = speed + step * (inverse[...] * (force[k] + dr2[k]) - (alive if k == 0 else 0.0))
        place2 = (place + step * speed2) * 0.0625
        for j in range(2):
            part[k, pl.ds(j, 16, stride=2), :] = place2[j * 16:(j + 1) * 16]
            part[2 + k, pl.ds(j, 16, stride=2), :] = speed2[j * 16:(j + 1) * 16]
    gas_step_update(gas, visc, gr, gc, dv, tot, rate, out)


CONTACT_SCRATCH = [
    pltpu.SMEM((128, 128), jnp.int32),
    pltpu.VMEM((128, 128), jnp.int32),
    pltpu.VMEM((128 * STRIDE, 128), F32),
    pltpu.VMEM((2, 1408, 128), F32),
    pltpu.VMEM((2, 64, 640), BF16),
    pltpu.VMEM((512, 128), F32),
]


def general(gas, visc, pos, vel, rad, coef, counts_t, pattern_t, idx, frac):

    def shapes(*dims):
        return [jax.ShapeDtypeStruct(d, F32) for d in dims]

    st, gp, mx = pl.pallas_call(
        prep_kernel,
        out_shape=shapes((8, 32, 128), (8, 32, 128), (8, 128)),
        in_specs=[VMEM_SPEC] * 5 + [SMEM_SPEC],
        out_specs=[VMEM_SPEC] * 3,
        name="prepare",
    )(gas, visc, pos, vel, rad, counts_t)
    ext, gv, rate, gr, gc = exchange(True, st, gp, mx, gas)
    st2, dp, tot, dr2, inverse = pl.pallas_call(
        first_kernel,
        out_shape=shapes((8, 32, 128), (8, 32, 128), (8, 128), (2, 32, 128), (32, 128)),
        in_specs=[VMEM_SPEC] * 6 + [SMEM_SPEC],
        out_specs=[VMEM_SPEC] * 5,
        scratch_shapes=CONTACT_SCRATCH + [pltpu.VMEM((2, 32, 128), F32), pltpu.SemaphoreType.DMA],
        name="first_substep",
    )(ext.reshape(1024, 128), gv, rate, idx, frac, coef, pattern_t)
    ext2, dv, total = exchange(False, st2, dp, tot)
    part, out = pl.pallas_call(
        second_kernel,
        out_shape=shapes((4, 32, 128), (2, 32, 256)),
        in_specs=[VMEM_SPEC] * 10 + [SMEM_SPEC],
        out_specs=[VMEM_SPEC] * 2,
        scratch_shapes=CONTACT_SCRATCH + [pltpu.SemaphoreType.DMA],
        name="second_substep",
    )(ext2.reshape(1024, 128), dv, total, rate, dr2, inverse, gas, visc, gr, gc, pattern_t)
    return part, out


EDGE_BASE, CORNER_BASE, WINDOW_ROWS = 48, 192, 256
CORNER = 16
WINDOWS = ((-1, 0), (1, 0), (0, -1), (0, 1), (-1, -1), (-1, 1), (1, -1), (1, 1))
NEAR = ((1.82, 0.0), (2.25, 0.43))
EDGE = 40


def fused_kernel(*refs):
    inputs, (part, out, flag, pat_copy, counts_copy), refs = refs[:10], refs[10:15], refs[15:]
    gas, visc, pos, vel, rad, coef, idx, frac, pat, counts = refs[:10]
    (in_sem, ext, ext2, gp, gv, dp, dv, gr, gc, mb, mv, sb, sv, rk, qs, qw, rhs, frc, itp, wts, wx, wz,
     hs, hr, ps, pr, rs, rr, es, er) = refs[10:]
    loads = [pltpu.make_async_copy(a, b, in_sem.at[n]) for n, (a, b) in enumerate(zip(inputs, refs[:10]))]
    for c in loads:
        c.start()
    ax, al, g = lax.axis_index("across"), lax.axis_index("along"), lax.axis_index("gas")

    def around(value, size):
        return value - jnp.where(value >= size, size, 0)

    up, down = around(al + 1, N_ALONG), around(al + N_ALONG - 1, N_ALONG)
    first_g, last_g = g == 0, g == N_GAS - 1
    has_left = jnp.logical_or(ax > 0, g > 0)
    has_right = jnp.logical_or(ax < N_ACROSS - 1, g < N_GAS - 1)
    left = (jnp.maximum(ax - jnp.where(first_g, 1, 0), 0), jnp.where(first_g, N_GAS - 1, g - 1))
    right = (jnp.minimum(ax + jnp.where(last_g, 1, 0), N_ACROSS - 1), jnp.where(last_g, 0, g + 1))

    def device(a=ax, l=al, y=g):
        return {"across": a, "along": l, "gas": y}

    def col(side, along):
        return device(a=side[0], l=along, y=side[1])

    def peer_id(axis, index):
        return device(**{{"across": "a", "along": "l", "gas": "y"}[axis]: index})

    after = device(l=jnp.where(last_g, up, al), y=jnp.where(last_g, 0, g + 1))
    before = device(l=jnp.where(first_g, down, al), y=jnp.where(first_g, N_GAS - 1, g - 1))

    barrier = pltpu.get_barrier_semaphore()

    def greet(target):
        pl.semaphore_signal(barrier, inc=1, device_id=target, device_id_type=MESH_ID)

    for k in range(1, N_ALONG):
        greet(device(l=around(al + k, N_ALONG)))
    for k in range(1, N_ACROSS):
        greet(device(a=around(ax + k, N_ACROSS)))
    for k in range(1, N_GAS):
        greet(device(y=around(g + k, N_GAS)))
    greet(after)
    greet(before)
    expect = N_ACROSS + N_GAS + N_ALONG - 3 + 2

    @pl.when(has_left)
    def _():
        for along in (down, al, up):
            greet(col(left, along))

    @pl.when(has_right)
    def _():
        for along in (down, al, up):
            greet(col(right, along))

    for c in loads:
        c.wait()
    rate = jnp.abs(gas[0]) + jnp.abs(gas[1]) + 4.0 * visc[...]
    top = jnp.max(jnp.max(rate, axis=1, keepdims=True), axis=0, keepdims=True)
    mv[0] = jnp.broadcast_to(top, (8, 128))
    lane = iota((16, 128), 1)
    for d in range(N_GAS):
        blk = slice((d // 4) * 128, (d // 4) * 128 + 128)
        off = (d % 4) * 32
        for k in range(2):
            low = gas[k, 0:16, blk]
            high = gas[k, 16:32, blk]
            low = pltpu.roll(low, (128 - off) % 128, 1) if off else low
            shift = (160 - off) % 128
            high = pltpu.roll(high, shift, 1) if shift else high
            piece = jnp.where(lane < 32, low, high)
            gp[d, k * 16:(k + 1) * 16, :] = jnp.where(lane < 64, piece, pltpu.roll(piece, 64, 1))
    row32 = iota((32, 128), 0)
    cnt = jnp.zeros((32, 128), jnp.int32)
    for j in range(2):
        for i in range(16):
            cnt = jnp.where(row32 == j * 16 + i, counts[j, i], cnt)
    ext[0, 0:32, :], ext[1, 0:32, :] = by_column(pos, 0) * 16.0, by_column(pos, 1) * 16.0
    ext[2, 0:32, :], ext[3, 0:32, :] = by_column(vel, 0), by_column(vel, 1)
    ext[4, 0:32, :] = jnp.where(iota((32, 128), 1) < cnt, by_column(rad), DEAD)

    def dots(e, low, high):
        e[5, low:high, :] = e[0, low:high, :] * e[2, low:high, :] + e[1, low:high, :] * e[3, low:high, :]

    dots(ext, 0, 32)
    for e in (ext, ext2):
        @pl.when(jnp.logical_not(has_left))
        def _():
            e[:, 32:48, :] = jnp.zeros((8, 16, 128), F32)
            e[:, 64:72, :] = jnp.zeros((8, 8, 128), F32)
            e[:, 96:104, :] = jnp.zeros((8, 8, 128), F32)

        @pl.when(jnp.logical_not(has_right))
        def _():
            e[:, 48:64, :] = jnp.zeros((8, 16, 128), F32)
            e[:, 88:96, :] = jnp.zeros((8, 8, 128), F32)
            e[:, 120:128, :] = jnp.zeros((8, 8, 128), F32)

    @pl.when(ax == 0)
    def _():
        gc[0] = jnp.zeros((2, 32, 128), F32)

    @pl.when(ax == N_ACROSS - 1)
    def _():
        gc[1] = jnp.zeros((2, 32, 128), F32)

    sides = jnp.where(has_left, 3, 0) + jnp.where(has_right, 3, 0)
    pl.semaphore_wait(barrier, expect + sides)

    def remote(src, dst, send, recv, target):
        return pltpu.make_async_remote_copy(
            src_ref=src, dst_ref=dst, send_sem=send, recv_sem=recv,
            device_id=target, device_id_type=MESH_ID,
        )

    axes = (("across", ax, N_ACROSS), ("gas", g, N_GAS), ("along", al, N_ALONG))

    def reduce_start(which, phase):
        slots, value = ((mb, mv), (sb, sv))[which]
        axis, me, size = axes[phase]
        out = [remote(value.at[phase], slots.at[phase, me], rs.at[which, phase, k], rr.at[which, phase, k],
                      peer_id(axis, around(me + k, size))) for k in range(1, size)]
        for c in out:
            c.start()
        slots[phase, me] = value[phase]
        return out

    def reduce_end(which, phase, copies):
        slots, value = ((mb, mv), (sb, sv))[which]
        size = axes[phase][2]
        for c in copies:
            c.wait_recv()
        total = slots[phase, 0]
        for k in range(1, size):
            total = total + slots[phase, k] if which else jnp.maximum(total, slots[phase, k])
        value[phase + 1] = total
        for c in copies:
            c.wait_send()

    def halo_start(which):
        e, attrs = ((ext, 5), (ext2, 5))[which]

        def halo(c, src_row, size, dst_row, target):
            return remote(e.at[pl.ds(0, attrs), pl.ds(src_row, size)],
                          e.at[pl.ds(0, attrs), pl.ds(dst_row, size)], hs.at[which, c], hr.at[which, c], target)

        lefts = [halo(0, 0, 16, 48, col(left, al)),
                 halo(1, 8, 8, 64 + 24, col(left, up)),
                 halo(2, 0, 8, 96 + 24, col(left, down))]
        rights = [halo(3, 16, 16, 32, col(right, al)),
                  halo(4, 24, 8, 64, col(right, up)),
                  halo(5, 16, 8, 96, col(right, down))]
        rows = [halo(6, 8, 8, 64 + 8, device(l=up)),
                halo(7, 24, 8, 64 + 16, device(l=up)),
                halo(8, 0, 8, 96 + 8, device(l=down)),
                halo(9, 16, 8, 96 + 16, device(l=down))]

        @pl.when(has_left)
        def _():
            for c in lefts:
                c.start()

        @pl.when(has_right)
        def _():
            for c in rights:
                c.start()

        for c in rows:
            c.start()
        return lefts, rights, rows

    def halo_end(copies):
        lefts, rights, rows = copies
        for c in rows:
            c.wait()

        @pl.when(has_left)
        def _():
            for c in lefts:
                c.wait_send()
            for c in rights:
                c.wait_recv()

        @pl.when(has_right)
        def _():
            for c in rights:
                c.wait_send()
            for c in lefts:
                c.wait_recv()

    def pieces_start(which):
        src, dst = ((gp, gv), (dp, dv))[which]
        out = []
        for k in range(1, N_GAS):
            peer = around(g + k, N_GAS)
            c = remote(src.at[peer], dst.at[g], ps.at[which, k], pr.at[which, k], device(y=peer))
            c.start()
            out.append(c)
        dst[g] = src[g]
        return out

    phase = reduce_start(0, 0)
    halos = halo_start(0)
    pieces = pieces_start(0)
    edges = [remote(gas.at[:, pl.ds(24, 8)], gr.at[0], es.at[0], er.at[0], after),
             remote(gas.at[:, pl.ds(0, 8)], gr.at[1], es.at[1], er.at[1], before)]
    for c in edges:
        c.start()
    to_right = remote(gas.at[:, :, pl.ds(128, 128)], gc.at[0], es.at[2], er.at[2],
                      device(a=jnp.minimum(ax + 1, N_ACROSS - 1)))
    to_left = remote(gas.at[:, :, pl.ds(0, 128)], gc.at[1], es.at[3], er.at[3],
                     device(a=jnp.maximum(ax - 1, 0)))

    @pl.when(ax < N_ACROSS - 1)
    def _():
        to_right.start()

    @pl.when(ax > 0)
    def _():
        to_left.start()

    lists = [pltpu.make_async_copy(pat, pat_copy, in_sem.at[10]), pltpu.make_async_copy(counts, counts_copy, in_sem.at[11])]
    for c in lists:
        c.start()

    slot_row = iota((48, 128), 0)
    slots = (jnp.where(slot_row < EDGE, slot_row, -5).astype(F32),
             jnp.where(slot_row < 32, slot_row, jnp.where(slot_row < 40, -5, slot_row - 8)).astype(F32))
    attr_row = iota((8, 128), 0)
    zero8 = jnp.zeros((8, 128), F32)
    one_tail = jnp.concatenate([zero8, jnp.ones((24, 128), F32)], axis=0)
    flat = (ext.reshape(1024, 128), ext2.reshape(1024, 128))
    eye = jnp.where(iota((128, 128), 0) == iota((128, 128), 1), 1.0, 0.0).astype(BF16)
    before_slot = jnp.where(iota((128, 128), 0) < iota((128, 128), 1), 1.0, 0.0).astype(BF16)

    def rank(which, low, high, windows=range(8)):
        e = (ext, ext2)[which]
        reach, _ = NEAR[which]
        z, x, live = e[0, low:high, :], e[1, low:high, :], e[4, low:high, :] > 0.0

        def flags(cond):
            return jnp.where(cond & live, 1.0, 0.0)

        lz, hz, lx, hx = flags(z < reach), flags(z > 16.0 - reach), flags(x < reach), flags(x > 16.0 - reach)
        member = [hz, lz, hx, lx, hz * hx, hz * lx, lz * hx, lz * lx]
        size = high - low
        places = jnp.dot(jnp.concatenate([member[w] for w in windows], axis=0).astype(BF16), before_slot,
                         preferred_element_type=F32)
        lost = jnp.zeros((size, 128), F32)
        for order, w in enumerate(windows):
            place = places[order * size:(order + 1) * size]
            rk[w, low:high, :] = jnp.where(member[w] > 0.0, place, -1.0)
            lost = lost + jnp.where(place >= (EDGE if w < 4 else CORNER), member[w], 0.0)
        return lost

    def parts(which, row):
        block = flat[which][pl.ds(row, 8, stride=128), :]
        return split3(jnp.where(attr_row < 6, block, 0.0))

    def stacked(hi, mid, lo):
        shifted = jnp.where(attr_row < 2, pltpu.roll(hi, 6, 0), jnp.where(attr_row < 4, mid, 0.0))
        return jnp.concatenate([hi, mid, lo, hi, mid, shifted, one_tail], axis=0)

    def partner(v):
        return jnp.where(attr_row < 2, pltpu.roll(v, 6, 0), jnp.where(attr_row < 4, pltpu.roll(v, 2, 0), 0.0))

    def window_rows(which, row, rows, windows):
        sizes = [48 if w < 4 else CORNER for w in windows]
        place = jnp.concatenate(
            [(slots[w & 1 if w < 4 else 0][0:n] == rk[w, pl.ds(row, 1), :]).astype(F32) for w, n in zip(windows, sizes)], axis=0)
        turned = lax.dot_general(place.astype(BF16), rows, (((1,), (1,)), ((), ())), preferred_element_type=F32)
        turned = turned.astype(BF16)
        at = 0
        for w, n in zip(windows, sizes):
            start = row * WINDOW_ROWS + (w * EDGE_BASE if w < 4 else CORNER_BASE + (w - 4) * CORNER)
            if not isinstance(row, int):
                start = pl.multiple_of(start, 16)
            qw[pl.ds(start, n), 0:80] = turned[at:at + n]
            at += n

    def own_tiles(which):
        def some(step, carry):
            for u in range(8):
                row = step * 8 + u
                hi, mid, lo = parts(which, row)
                rows = stacked(hi, mid, lo)
                turned = rows.T
                rows = rows.astype(BF16)
                qs[pl.ds(pl.multiple_of(row * 128, 128), 128), 0:80] = turned.astype(BF16)
                window_rows(which, row, rows, range(8))
                with_hi, with_mid = 2.0 * partner(hi), 2.0 * partner(mid)
                own = jnp.where(attr_row == 5, -2.0, with_hi)
                marked = 16.0 * jnp.where(attr_row < 2, with_hi, jnp.where(attr_row < 4, pltpu.roll(with_mid, 2, 0), 0.0))
                columns = []
                for a, scale in ((0, 1.0), (1, 1.0), (5, -2.0), (4, 1.0)):
                    ends = [jnp.where(attr_row == a, v * scale, 0.0) for v in (hi, mid, lo)]
                    if a == 5:
                        start = [own, own, jnp.where(attr_row == 5, -2.0, 0.0), with_mid, with_mid,
                                 jnp.where(attr_row < 4, -32.0, 0.0), marked]
                    else:
                        one = jnp.where(attr_row == a, 1.0 if a == 4 else -1.0, 0.0)
                        start = [one, one, one, zero8, zero8, zero8,
                                 jnp.where(attr_row == a, DEAD if a == 4 else -16.0, 0.0)]
                    columns.append(jnp.concatenate(start + ends, axis=0))
                rhs[row] = jnp.concatenate(columns, axis=1).astype(BF16)
            return carry
        lax.fori_loop(0, 4, some, 0)

    def halo_tile(which, row, windows):
        hi, mid, lo = parts(which, row)
        window_rows(which, row, stacked(hi, mid, lo).astype(BF16), windows)

    def halo_tiles(which, beside=None):
        dots((ext, ext2)[which], 32, 128)
        rank(which, 32, 48, (2, 4, 6))
        rank(which, 48, 64, (3, 5, 7))
        rank(which, 64, 96, (0, 4, 5))
        rank(which, 96, 128, (1, 6, 7))

        def some(step, carry):
            if beside is not None:
                beside(step)
            for u in range(4):
                halo_tile(which, 32 + step * 4 + u, (2, 4, 6))
                halo_tile(which, 48 + step * 4 + u, (3, 5, 7))
            return carry
        lax.fori_loop(0, 4, some, 0)
        for c in range(4):
            halo_tile(which, 64 + 8 * c + 7, (0, 4, 5))
            halo_tile(which, 96 + 8 * c, (1, 6, 7))

    lane16 = iota((16, 128), 1)
    half = iota((16, 128), 0) < 8

    lost = rank(0, 0, 32)
    own_tiles(0)
    index = idx[...]
    share_z = frac[0].astype(F32) / 1024.0
    share_x = frac[1].astype(F32) / 1024.0
    wts[0] = (index >> 4).astype(F32)
    wts[1] = (index & 15).astype(F32)
    wts[2], wts[3] = 1.0 - share_z, share_z
    for n, share in ((4, 1.0 - share_x), (6, share_x)):
        high = share.astype(BF16).astype(F32)
        wts[n], wts[n + 1] = high, share - high
    c64 = iota((64, 128), 0).astype(F32)
    r16 = iota((16, 128), 0).astype(F32)

    def weigh(r, t4, t):
        def get(n):
            return wts[n, pl.ds(r, 1), :]
        column, row = get(1) + (16.0 * t4), get(0)
        here, there = c64 == column, c64 == column + 1.0
        wx[t, 0:64, :] = jnp.where(here, get(4), jnp.where(there, get(6), 0.0)).astype(BF16)
        wx[t, 64:128, :] = jnp.where(here, get(5), jnp.where(there, get(7), 0.0)).astype(BF16)
        wz[t] = jnp.where(r16 == row, get(2), jnp.where(r16 == row + 1.0, get(3), 0.0))

    def some_weights(h, carry):
        for t in range(2):
            for j in range(2):
                weigh(4 * h + 2 * t + j, t * 2 + j, 4 * h + 2 * t + j)
        return carry

    lax.fori_loop(0, 8, some_weights, 0)

    unlisted = jnp.where(lane16 == 52, 1.0, 0.0)

    def by_offset(low, di, dj, rest):
        lane = lane16 - low
        inside = (lane >= 0) & (lane < 4)
        return jnp.where(inside, jnp.where((lane & 1) == 0, float(di), float(dj)), rest)

    def contact_rows(first, last):

        def step(two, carry):
            for j, u in ((0, 0), (1, 0), (0, 1), (1, 1)):
                i = two * 2 + u
                t = j * 16 + i
                right = rhs[t]

                def mark_of(n):
                    di, dj = OFFSETS[n]
                    base = by_offset(48, di, dj, 0.0)
                    return base + unlisted * (1 - pat[n, j, i]).astype(F32)

                def times(di, dj):
                    return by_offset(40, di, dj, 1.0).astype(BF16)

                def border(w):
                    di, dj = WINDOWS[w]
                    row = ext_row(i + di, j + dj)
                    n = 48 if w < 4 else CORNER
                    start = row * WINDOW_ROWS + (w * EDGE_BASE if w < 4 else CORNER_BASE + (w - 4) * CORNER)
                    block, factor = qw[pl.ds(pl.multiple_of(start, 16), n), :], times(di, dj)
                    return [block[c:c + 16] * factor for c in range(0, n, 16)], mark_of(3 * (di + 1) + dj + 1)

                def edges_of(w):
                    (one, mark1), (two, mark2) = border(w), border(w + 1)
                    both = one[2] + two[2] + jnp.where(half, mark1, mark2).astype(BF16)
                    mark1, mark2 = mark1.astype(BF16), mark2.astype(BF16)
                    return [one[0] + mark1, one[1] + mark1, two[0] + mark2, two[1] + mark2, both]

                def corner(w):
                    (block,), here = border(w)
                    return block + here.astype(BF16)

                own = qs[pl.ds(pl.multiple_of(t * 128, 128), 128), :]
                factor, here = times(0, 0), mark_of(4).astype(BF16)
                groups = [own[c:c + 16] * factor + here for c in range(0, 128, 16)]
                groups += edges_of(0) + edges_of(2) + [corner(w) for w in range(4, 8)]
                got = jnp.dot(jnp.concatenate(groups, axis=0)[:, 0:80], right, preferred_element_type=F32)
                rz, rx = got[:, 0:128], got[:, 128:256]
                inv = lax.rsqrt(rz * rz + rx * rx + 0.0001)
                push = jnp.maximum(got[:, 384:512] * inv - 1.0, 0.0) * (40.0 + got[:, 256:384] * inv)
                count = got.shape[0] // 8
                fz = jnp.sum((push * rz).reshape(count, 8, 128), axis=0)
                fx = jnp.sum((push * rx).reshape(count, 8, 128), axis=0)
                frc[pl.ds(pl.multiple_of(t * 8, 8), 8), :] = fz
                frc[pl.ds(pl.multiple_of(t * 8 + 256, 8), 8), :] = fx
            return carry
        lax.fori_loop(first // 2, last // 2, step, 0)

    def forces():
        return [sum(frc[pl.ds(k * 256 + r, 32, stride=8), :] for r in range(8)) for k in range(2)]

    phase_end = reduce_end
    for c in pieces:
        c.wait()
    lane32 = iota((32, 128), 1)

    def sample(h):
        field = gv[h]
        high = field.astype(BF16).astype(F32)
        both = jnp.where(lane32 < 64, high, field - high).astype(BF16)
        for t in range(2):
            for j in range(2):
                r = 4 * h + 2 * t + j
                whi, wlo = wx[r, 0:64, :], wx[r, 64:128, :]
                right = jnp.concatenate([jnp.concatenate([whi, whi], axis=0),
                                         jnp.concatenate([wlo, wlo], axis=0)], axis=1)
                got = jnp.dot(both, right, preferred_element_type=F32)
                got = got[:, 0:128] + got[:, 128:256]
                for k in range(2):
                    itp[k, pl.ds(j * 16 + 2 * h + t, 1), :] = jnp.sum(
                        wz[r] * got[k * 16:(k + 1) * 16], axis=0, keepdims=True)

    def two_samples(step):
        sample(2 * step)
        sample(2 * step + 1)

    phase_end(0, 0, phase)
    phase = reduce_start(0, 1)
    halo_end(halos)
    halo_tiles(0, two_samples)

    contact_rows(0, 4)
    phase_end(0, 1, phase)
    phase = reduce_start(0, 2)
    contact_rows(4, 16)
    phase_end(0, 2, phase)
    step = 0.2 / mv[3][0:1, :]
    drag = by_column(coef)
    radius = ext[4, 0:32, :]
    alive = jnp.where(radius > 0.0, 1.0, 0.0)
    inverse = jnp.where(radius > 0.0, 0.36 / (radius * radius), 0.0)
    force = forces()
    drags = []
    slack = NEAR[1][1]
    for k in range(2):
        speed = ext[2 + k, 0:32, :]
        drag1 = drag * (itp[k] - speed)
        speed2 = speed + step * (inverse * (force[k] + drag1) - (alive if k == 0 else 0.0))
        place2 = ext[k, 0:32, :] + step * speed2
        ext2[k, 0:32, :] = place2
        inside = (place2 >= -slack) & (place2 <= 16.0 + slack)
        lost = lost + jnp.where(inside, 0.0, alive)
        ext2[2 + k, 0:32, :] = speed2
        drag2 = drag * (itp[k] - speed2)
        drags.append((drag1, drag2))
    ext2[4, 0:32, :] = radius
    dots(ext2, 0, 32)
    halos = halo_start(1)
    bad = lost + rank(1, 0, 32)
    sums = []
    for k in range(2):
        drag1, drag2 = drags[k]
        mean = 0.5 * (alive * drag1 + alive * drag2)
        itp[k] = mean
        itp[2 + k] = drag2
        sums.append(jnp.sum(jnp.sum(mean, axis=1, keepdims=True), axis=0, keepdims=True))
    bad = jnp.sum(jnp.sum(bad, axis=1, keepdims=True), axis=0, keepdims=True)
    sv[0] = jnp.where(attr_row == 0, sums[0], jnp.where(attr_row == 1, sums[1], bad))
    phase = reduce_start(1, 0)

    def spread(h):
        total = jnp.zeros((64, 128), F32)
        for t in range(2):
            for j in range(2):
                r = 4 * h + 2 * t + j
                m0 = itp[0, pl.ds(j * 16 + 2 * h + t, 1), :]
                m1 = itp[1, pl.ds(j * 16 + 2 * h + t, 1), :]
                lhs = jnp.concatenate([wz[r] * m0, wz[r] * m1], axis=0)
                high = lhs.astype(BF16)
                low = (lhs - high.astype(F32)).astype(BF16)
                total = total + lax.dot_general(
                    jnp.concatenate([high, low], axis=0), wx[r],
                    (((1,), (1,)), ((), ())), preferred_element_type=F32)
        total = total[0:32] + total[32:64]
        dp[h] = total + pltpu.roll(total, 64, 1)

    lax.fori_loop(0, 8, lambda h, carry: (spread(h), carry)[1], 0)
    pieces = pieces_start(1)
    own_tiles(1)
    phase_end(1, 0, phase)
    phase = reduce_start(1, 1)
    halo_end(halos)
    halo_tiles(1)

    contact_rows(0, 4)
    phase_end(1, 1, phase)
    phase = reduce_start(1, 2)
    contact_rows(4, 16)
    force = forces()
    for k in range(2):
        speed = ext2[2 + k, 0:32, :]
        speed2 = speed + step * (inverse * (force[k] + itp[2 + k]) - (alive if k == 0 else 0.0))
        place2 = (ext2[k, 0:32, :] + step * speed2) * 0.0625
        for j in range(2):
            part[k, pl.ds(j, 16, stride=2), :] = place2[j * 16:(j + 1) * 16]
            part[2 + k, pl.ds(j, 16, stride=2), :] = speed2[j * 16:(j + 1) * 16]
    for c in edges + lists:
        c.wait()

    @pl.when(ax < N_ACROSS - 1)
    def _():
        to_right.wait_send()
        to_left.wait_recv()

    @pl.when(ax > 0)
    def _():
        to_left.wait_send()
        to_right.wait_recv()

    for c in pieces:
        c.wait()
    phase_end(1, 2, phase)
    flag[...] = sv[3][2:3, 0:1]
    gas_step_update(gas, visc, gr, gc, dv, sv.at[3], mv.at[3], out)


def fused(gas, visc, pos, vel, rad, coef, counts_t, pattern_t, idx, frac):
    dma = pltpu.SemaphoreType.DMA
    return pl.pallas_call(
        fused_kernel,
        out_shape=[jax.ShapeDtypeStruct((4, 32, 128), F32), jax.ShapeDtypeStruct((2, 32, 256), F32),
                   jax.ShapeDtypeStruct((1, 1), F32), jax.ShapeDtypeStruct((9, 2, 16), jnp.int32),
                   jax.ShapeDtypeStruct((2, 16), jnp.int32)],
        in_specs=[pl.BlockSpec(memory_space=pltpu.HBM)] * 10,
        out_specs=[VMEM_SPEC] * 3 + [pl.BlockSpec(memory_space=pltpu.HBM)] * 2,
        scratch_shapes=[
            pltpu.VMEM((2, 32, 256), F32), pltpu.VMEM((32, 256), F32),
            pltpu.VMEM((2, 32, 128), F32), pltpu.VMEM((2, 32, 128), F32), pltpu.VMEM((32, 128), F32),
            pltpu.VMEM((32, 128), F32), pltpu.VMEM((32, 128), jnp.int32), pltpu.VMEM((2, 32, 128), jnp.int32),
            pltpu.SMEM((9, 2, 16), jnp.int32), pltpu.SMEM((2, 16), jnp.int32), dma((12,)),
            pltpu.VMEM((8, 128, 128), F32), pltpu.VMEM((8, 128, 128), F32),
            pltpu.VMEM((8, 32, 128), F32), pltpu.VMEM((8, 32, 128), F32),
            pltpu.VMEM((8, 32, 128), F32), pltpu.VMEM((8, 32, 128), F32),
            pltpu.VMEM((2, 2, 8, 256), F32), pltpu.VMEM((2, 2, 32, 128), F32),
            pltpu.VMEM((3, 8, 8, 128), F32), pltpu.VMEM((4, 8, 128), F32),
            pltpu.VMEM((3, 8, 8, 128), F32), pltpu.VMEM((4, 8, 128), F32),
            pltpu.VMEM((8, 128, 128), F32), pltpu.VMEM((32 * 128, 128), BF16),
            pltpu.VMEM((128 * WINDOW_ROWS, 128), BF16), pltpu.VMEM((32, 80, 512), BF16),
            pltpu.VMEM((512, 128), F32), pltpu.VMEM((4, 32, 128), F32), pltpu.VMEM((8, 32, 128), F32),
            pltpu.VMEM((32, 128, 128), BF16), pltpu.VMEM((32, 16, 128), F32),
            dma((2, 10)), dma((2, 10)), dma((2, 8)), dma((2, 8)), dma((2, 3, 8)), dma((2, 3, 8)),
            dma((4,)), dma((4,)),
        ],
        compiler_params=pltpu.CompilerParams(collective_id=2, has_side_effects=True),
        name="interval",
    )(gas, visc, pos, vel, rad, coef, idx, frac, pattern_t, counts_t)


def body(gas, visc, pos, vel, rad, coef, counts, pattern, idx, frac):
    pos, vel, frac = (x.reshape(2, 32, 128) for x in (pos, vel, frac))
    rad, coef, idx = (x.reshape(32, 128) for x in (rad, coef, idx))
    args = (gas, visc, pos, vel, rad, coef, counts.T, pattern.transpose(2, 1, 0), idx, frac)
    part, out, flag, pattern_t, counts_t = fused(*args)
    args = args[:6] + (counts_t, pattern_t) + args[8:]
    part, out = lax.cond(flag[0, 0] > 0.0, lambda p, o: tuple(general(*args)), lambda p, o: (p, o), part, out)
    return part.reshape(4, 16, 2, 128), out


def solution(mesh):
    return jax.shard_map(
        body,
        mesh=mesh,
        in_specs=(
            P(None, ALONG_GAS, "across"),
            P(ALONG_GAS, "across"),
            P(None, "along", ACROSS_GAS, None),
            P(None, "along", ACROSS_GAS, None),
            P("along", ACROSS_GAS, None),
            P("along", ACROSS_GAS, None),
            P("along", ACROSS_GAS),
            P("along", ACROSS_GAS, None),
            P("along", ACROSS_GAS, None),
            P(None, "along", ACROSS_GAS, None),
        ),
        out_specs=(P(None, "along", ACROSS_GAS, None), P(None, ALONG_GAS, "across")),
        check_vma=False,
    )
```

profile of v0, /device:TPU:81, one launch (start us, length us, event | category | flops | bytes accessed | tf_op | source)
XLA Modules:
  0.0 138.7 jit_solution(11305509507173408377)
XLA Ops:
  0.6 0.0 copy-start
  0.6 0.0 copy-start.1
  0.7 0.0 copy-start.2
  0.7 0.0 copy-start.3
  0.7 0.0 copy-start.4
  0.7 0.0 copy-start.6
  0.7 0.0 copy-start.7
  0.7 33.0 %interval.1 = (f32[4,32,128]{2,1,0:T(8,128)S(1)}, f32[2,32,256]{2,1,0:T(8,128)S(1)}, f32[1,1]{1,0:T(1,128)}, s32[9,2,16]{2,1,0:T(2,128)S(1)}, s32[2,16]{1,0:T(2,128)S(1)}) custom-call(f32[2,32,256]{2,1,0:T(8,128)} %refs_0_.1, f32[32,256]{1,0:T(8,128)} %refs_1_.1, f32[2,32,128]{2,1,0:T(8,128)} %bitcast.16, f32[2,32,128]{2,1,0:T(8,128)} %bitcast.18, ...), custom_call_target="tpu_custom_call" | custom-call | tf_op jit(solution)/shard_map/interval/pallas_call | solution.py:1178
  33.7 0.0 copy-start.5
  34.3 0.0 copy-done
  34.3 0.0 copy-done.1
  34.4 0.0 copy-done.2
  34.4 0.0 copy-done.3
  34.4 0.0 copy-done.4
  34.4 0.0 copy-done.6
  34.4 0.0 copy-done.7
  34.4 0.0 copy-done.5
  34.4 103.0 %conditional.1 = ((f32[2,32,256]{2,1,0:T(8,128)S(1)}, f32[4,32,128]{2,1,0:T(8,128)S(1)})) conditional(s32[]{:T(128)} %bitcast.10, (f32[2,32,256]{2,1,0:T(8,128)S(1)}, f32[4,32,128]{2,1,0:T(8,128)S(1)}) %tuple.20, (f32[2,32,256]{2,1,0:T(8,128)S(1)}, f32[32,256]{1,0:T(8,128)S(1)}, f32[2,32,128]{2,1,0:T(8,128)S(1)}, f32[2,32,128]{2,1,0:T(8,128)S(1)}, ...), branch_computations={%region_0.0_spmd, %region_1.0_spmd} | conditional | bytes 24 | solution.py:1214
  34.4 1.5 %prepare.1 = (f32[8,32,128]{2,1,0:T(8,128)}, f32[8,32,128]{2,1,0:T(8,128)}, f32[8,128]{1,0:T(8,128)}) custom-call(f32[2,32,256]{2,1,0:T(8,128)S(1)} %get-tuple-element.31.gas.refs_3_, f32[32,256]{1,0:T(8,128)S(1)} %get-tuple-element.32.visc, f32[2,32,128]{2,1,0:T(8,128)S(1)} %get-tuple-element.33.pos, f32[2,32,128]{2,1,0:T(8,128)S(1)} %get-tuple-element.34.vel, ...), custom_call_target="tpu_custom_call" | custom-call | tf_op jit(solution)/shard_map/cond/branch_1_fun/prepare/pallas_call | solution.py:589
  35.9 17.9 %exchange_first.1 = (f32[8,128,128]{2,1,0:T(8,128)}, f32[8,32,128]{2,1,0:T(8,128)}, f32[8,128]{1,0:T(8,128)}, f32[2,2,8,256]{3,2,1,0:T(8,128)}, f32[2,2,32,128]{3,2,1,0:T(8,128)}) custom-call(f32[8,32,128]{2,1,0:T(8,128)} %get-tuple-element.37.refs_0_, f32[8,32,128]{2,1,0:T(8,128)} %get-tuple-element.38.refs_1_, f32[8,128]{1,0:T(8,128)} %get-tuple-element.39.refs_2_, ...), custom_call_target="tpu_custom_call" | custom-call | tf_op jit(solution)/shard_map/cond/branch_1_fun/exchange_first/pallas_call | solution.py:315
  53.8 27.1 %first_substep.1 = (f32[8,32,128]{2,1,0:T(8,128)}, f32[8,32,128]{2,1,0:T(8,128)}, f32[8,128]{1,0:T(8,128)}, f32[2,32,128]{2,1,0:T(8,128)}, f32[32,128]{1,0:T(8,128)}) custom-call(f32[1024,128]{1,0:T(8,128)} %bitcast.13, f32[8,32,128]{2,1,0:T(8,128)} %get-tuple-element.41.gv, f32[8,128]{1,0:T(8,128)} %get-tuple-element.42.rate, ...), custom_call_target="tpu_custom_call" | custom-call | tf_op jit(solution)/shard_map/cond/branch_1_fun/first_substep/pallas_call | solution.py:597
  80.9 15.6 %exchange_second.1 = (f32[8,128,128]{2,1,0:T(8,128)}, f32[8,32,128]{2,1,0:T(8,128)}, f32[8,128]{1,0:T(8,128)}) custom-call(f32[8,32,128]{2,1,0:T(8,128)} %get-tuple-element.47.refs_0_, f32[8,32,128]{2,1,0:T(8,128)} %get-tuple-element.48.refs_1_, f32[8,128]{1,0:T(8,128)} %get-tuple-element.49.refs_2_), custom_call_target="tpu_custom_call" | custom-call | tf_op jit(solution)/shard_map/cond/branch_1_fun/exchange_second/pallas_call | solution.py:315
  96.5 40.9 %second_substep.1 = (f32[4,32,128]{2,1,0:T(8,128)S(1)}, f32[2,32,256]{2,1,0:T(8,128)S(1)}) custom-call(f32[1024,128]{1,0:T(8,128)} %bitcast.12, f32[8,32,128]{2,1,0:T(8,128)} %get-tuple-element.51.dv, f32[8,128]{1,0:T(8,128)} %get-tuple-element.52.tot, f32[8,128]{1,0:T(8,128)} %get-tuple-element.42.rate, f32[2,32,128]{2,1,0:T(8,128)} %get-tuple-element.53.dr2, ...), custom_call_target="tpu_custom_call" | custom-call | tf_op jit(solution)/shard_map/cond/branch_1_fun/second_substep/pallas_call | solution.py:606
  137.4 0.6 copy.18
  138.0 0.6 copy.19
Async XLA Ops:
  0.6 33.7 %copy-start = (f32[2,32,256]{2,1,0:T(8,128)S(1)}, f32[2,32,256]{2,1,0:T(8,128)}, u32[]{:S(2)}) copy-start(f32[2,32,256]{2,1,0:T(8,128)} %refs_0_.1) | copy-start | bytes 196612
  0.6 33.7 %copy-start.1 = (f32[32,256]{1,0:T(8,128)S(1)}, f32[32,256]{1,0:T(8,128)}, u32[]{:S(2)}) copy-start(f32[32,256]{1,0:T(8,128)} %refs_1_.1) | copy-start | bytes 98308
  0.7 33.7 %copy-start.2 = (s32[2,16,2,128]{3,2,1,0:T(2,128)S(1)}, s32[2,16,2,128]{3,2,1,0:T(2,128)}, u32[]{:S(2)}) copy-start(s32[2,16,2,128]{3,2,1,0:T(2,128)} %param.21) | copy-start | bytes 98308
  0.7 33.7 %copy-start.3 = (f32[2,16,2,128]{3,2,1,0:T(2,128)S(1)}, f32[2,16,2,128]{3,2,1,0:T(2,128)}, u32[]{:S(2)}) copy-start(f32[2,16,2,128]{3,2,1,0:T(2,128)} %param.14) | copy-start | bytes 98308
  0.7 33.7 %copy-start.4 = (f32[2,16,2,128]{3,2,1,0:T(2,128)S(1)}, f32[2,16,2,128]{3,2,1,0:T(2,128)}, u32[]{:S(2)}) copy-start(f32[2,16,2,128]{3,2,1,0:T(2,128)} %param.15) | copy-start | bytes 98308
  0.7 33.7 %copy-start.6 = (s32[16,2,128]{2,1,0:T(2,128)S(1)}, s32[16,2,128]{2,1,0:T(2,128)}, u32[]{:S(2)}) copy-start(s32[16,2,128]{2,1,0:T(2,128)} %param.20) | copy-start | bytes 49156
  0.7 33.7 %copy-start.7 = (f32[16,2,128]{2,1,0:T(2,128)S(1)}, f32[16,2,128]{2,1,0:T(2,128)}, u32[]{:S(2)}) copy-start(f32[16,2,128]{2,1,0:T(2,128)} %param.16) | copy-start | bytes 49156
  33.7 0.7 copy-start.5
where the time goes:
time: 136 us; the launch traced here: 139 us
  Pallas kernels  136 us (100%)
  between operations  1.43 us (1%)
    pallas_call x1, Pallas kernels, general(): pl.pallas_call(second_kernel, out_shape=shapes((4, 32, 128), (2, 32, 256)...  40.9 us
    pallas_call x2, Pallas kernels, exchange(): pl.pallas_call(functools.partial(comm_kernel, first), out_shape=out_shape...  33.5 us
    pallas_call x1, Pallas kernels, fused(): pl.pallas_call(fused_kernel, out_shape=[jax.ShapeDtypeStruct((4, 32, 128)...  33 us
    pallas_call x1, Pallas kernels, general(): pl.pallas_call(first_kernel, out_shape=shapes((8, 32, 128), (8, 32, 128),...  27.1 us

commit v1 on v0

--- a/solution.py
+++ b/solution.py
@@ -619,6 +619,7 @@
 WINDOWS = ((-1, 0), (1, 0), (0, -1), (0, 1), (-1, -1), (-1, 1), (1, -1), (1, 1))
 NEAR = ((1.82, 0.0), (2.25, 0.43))
 EDGE = 40
+EARLY = 8
 
 
 def fused_kernel(*refs):
@@ -882,9 +883,9 @@
         block = flat[which][pl.ds(row, 8, stride=128), :]
         return split3(jnp.where(attr_row < 6, block, 0.0))
 
-    def stacked(hi, mid, lo):
+    def stacked(hi, mid, lo, own=False):
         shifted = jnp.where(attr_row < 2, pltpu.roll(hi, 6, 0), jnp.where(attr_row < 4, mid, 0.0))
-        return jnp.concatenate([hi, mid, lo, hi, mid, shifted, one_tail], axis=0)
+        return jnp.concatenate([hi, mid, lo, hi, mid, zero8 if own else shifted, one_tail], axis=0)
 
     def partner(v):
         return jnp.where(attr_row < 2, pltpu.roll(v, 6, 0), jnp.where(attr_row < 4, pltpu.roll(v, 2, 0), 0.0))
@@ -908,9 +909,8 @@
             for u in range(8):
                 row = step * 8 + u
                 hi, mid, lo = parts(which, row)
-                rows = stacked(hi, mid, lo)
-                turned = rows.T
-                rows = rows.astype(BF16)
+                turned = stacked(hi, mid, lo, True).T
+                rows = stacked(hi, mid, lo).astype(BF16)
                 qs[pl.ds(pl.multiple_of(row * 128, 128), 128), 0:80] = turned.astype(BF16)
                 window_rows(which, row, rows, range(8))
                 with_hi, with_mid = 2.0 * partner(hi), 2.0 * partner(mid)
@@ -959,6 +959,73 @@
 
     lost = rank(0, 0, 32)
     own_tiles(0)
+
+    unlisted = jnp.where(lane16 == 52, 1.0, 0.0)
+
+    def by_offset(low, di, dj, rest):
+        lane = lane16 - low
+        inside = (lane >= 0) & (lane < 4)
+        return jnp.where(inside, jnp.where((lane & 1) == 0, float(di), float(dj)), rest)
+
+    def contact_rows(first, last, own_part=True, border_part=True):
+
+        def step(four, carry):
+            for u, j in ((0, 0), (0, 1), (1, 0), (1, 1), (2, 0), (2, 1), (3, 0), (3, 1)):
+                i = four * 4 + u
+                t = j * 16 + i
+                right = rhs[t]
+
+                def mark_of(n):
+                    di, dj = OFFSETS[n]
+                    base = by_offset(48, di, dj, 0.0)
+                    return base + unlisted * (1 - pat[n, j, i]).astype(F32)
+
+                def times(di, dj):
+                    return by_offset(40, di, dj, 1.0).astype(BF16)
+
+                def border(w):
+                    di, dj = WINDOWS[w]
+                    row = ext_row(i + di, j + dj)
+                    n = 48 if w < 4 else CORNER
+                    start = row * WINDOW_ROWS + (w * EDGE_BASE if w < 4 else CORNER_BASE + (w - 4) * CORNER)
+                    block, factor = qw[pl.ds(pl.multiple_of(start, 16), n), :], times(di, dj)
+                    return [block[c:c + 16] * factor for c in range(0, n, 16)], mark_of(3 * (di + 1) + dj + 1)
+
+                def edges_of(w):
+                    (one, mark1), (two, mark2) = border(w), border(w + 1)
+                    both = one[2] + two[2] + jnp.where(half, mark1, mark2).astype(BF16)
+                    mark1, mark2 = mark1.astype(BF16), mark2.astype(BF16)
+                    return [one[0] + mark1, one[1] + mark1, two[0] + mark2, two[1] + mark2, both]
+
+                def corner(w):
+                    (block,), here = border(w)
+                    return block + here.astype(BF16)
+
+                groups = []
+                if own_part:
+                    own = qs[pl.ds(pl.multiple_of(t * 128, 128), 128), :]
+                    here = mark_of(4).astype(BF16)
+                    groups += [own[c:c + 16] + here for c in range(0, 128, 16)]
+                if border_part:
+                    groups += edges_of(0) + edges_of(2) + [corner(w) for w in range(4, 8)]
+                got = jnp.dot(jnp.concatenate(groups, axis=0)[:, 0:80], right, preferred_element_type=F32)
+                rz, rx = got[:, 0:128], got[:, 128:256]
+                inv = lax.rsqrt(rz * rz + rx * rx + 0.0001)
+                push = jnp.maximum(got[:, 384:512] * inv - 1.0, 0.0) * (40.0 + got[:, 256:384] * inv)
+                count = got.shape[0] // 8
+                fz = jnp.sum((push * rz).reshape(count, 8, 128), axis=0)
+                fx = jnp.sum((push * rx).reshape(count, 8, 128), axis=0)
+                at_z, at_x = pl.ds(pl.multiple_of(t * 8, 8), 8), pl.ds(pl.multiple_of(t * 8 + 256, 8), 8)
+                if not own_part:
+                    fz, fx = fz + frc[at_z, :], fx + frc[at_x, :]
+                frc[at_z, :], frc[at_x, :] = fz, fx
+            return carry
+        lax.fori_loop(first // 4, last // 4, step, 0)
+
+    def forces():
+        return [sum(frc[pl.ds(k * 256 + r, 32, stride=8), :] for r in range(8)) for k in range(2)]
+
+    phase_end = reduce_end
     index = idx[...]
     share_z = frac[0].astype(F32) / 1024.0
     share_x = frac[1].astype(F32) / 1024.0
@@ -987,68 +1054,8 @@
         return carry
 
     lax.fori_loop(0, 8, some_weights, 0)
-
-    unlisted = jnp.where(lane16 == 52, 1.0, 0.0)
-
-    def by_offset(low, di, dj, rest):
-        lane = lane16 - low
-        inside = (lane >= 0) & (lane < 4)
-        return jnp.where(inside, jnp.where((lane & 1) == 0, float(di), float(dj)), rest)
-
-    def contact_rows(first, last):
-
-        def step(two, carry):
-            for j, u in ((0, 0), (1, 0), (0, 1), (1, 1)):
-                i = two * 2 + u
-                t = j * 16 + i
-                right = rhs[t]
-
-                def mark_of(n):
-                    di, dj = OFFSETS[n]
-                    base = by_offset(48, di, dj, 0.0)
-                    return base + unlisted * (1 - pat[n, j, i]).astype(F32)
-
-                def times(di, dj):
-                    return by_offset(40, di, dj, 1.0).astype(BF16)
-
-                def border(w):
-                    di, dj = WINDOWS[w]
-                    row = ext_row(i + di, j + dj)
-                    n = 48 if w < 4 else CORNER
-                    start = row * WINDOW_ROWS + (w * EDGE_BASE if w < 4 else CORNER_BASE + (w - 4) * CORNER)
-                    block, factor = qw[pl.ds(pl.multiple_of(start, 16), n), :], times(di, dj)
-                    return [block[c:c + 16] * factor for c in range(0, n, 16)], mark_of(3 * (di + 1) + dj + 1)
-
-                def edges_of(w):
-                    (one, mark1), (two, mark2) = border(w), border(w + 1)
-                    both = one[2] + two[2] + jnp.where(half, mark1, mark2).astype(BF16)
-                    mark1, mark2 = mark1.astype(BF16), mark2.astype(BF16)
-                    return [one[0] + mark1, one[1] + mark1, two[0] + mark2, two[1] + mark2, both]
-
-                def corner(w):
-                    (block,), here = border(w)
-                    return block + here.astype(BF16)
-
-                own = qs[pl.ds(pl.multiple_of(t * 128, 128), 128), :]
-                factor, here = times(0, 0), mark_of(4).astype(BF16)
-                groups = [own[c:c + 16] * factor + here for c in range(0, 128, 16)]
-                groups += edges_of(0) + edges_of(2) + [corner(w) for w in range(4, 8)]
-                got = jnp.dot(jnp.concatenate(groups, axis=0)[:, 0:80], right, preferred_element_type=F32)
-                rz, rx = got[:, 0:128], got[:, 128:256]
-                inv = lax.rsqrt(rz * rz + rx * rx + 0.0001)
-                push = jnp.maximum(got[:, 384:512] * inv - 1.0, 0.0) * (40.0 + got[:, 256:384] * inv)
-                count = got.shape[0] // 8
-                fz = jnp.sum((push * rz).reshape(count, 8, 128), axis=0)
-                fx = jnp.sum((push * rx).reshape(count, 8, 128), axis=0)
-                frc[pl.ds(pl.multiple_of(t * 8, 8), 8), :] = fz
-                frc[pl.ds(pl.multiple_of(t * 8 + 256, 8), 8), :] = fx
-            return carry
-        lax.fori_loop(first // 2, last // 2, step, 0)
-
-    def forces():
-        return [sum(frc[pl.ds(k * 256 + r, 32, stride=8), :] for r in range(8)) for k in range(2)]
-
-    phase_end = reduce_end
+    contact_rows(0, EARLY, True, False)
+
     for c in pieces:
         c.wait()
     lane32 = iota((32, 128), 1)
@@ -1078,10 +1085,10 @@
     halo_end(halos)
     halo_tiles(0, two_samples)
 
-    contact_rows(0, 4)
+    contact_rows(0, EARLY, False, True)
     phase_end(0, 1, phase)
     phase = reduce_start(0, 2)
-    contact_rows(4, 16)
+    contact_rows(EARLY, 16)
     phase_end(0, 2, phase)
     step = 0.2 / mv[3][0:1, :]
     drag = by_column(coef)

time: 136 us -> 136 us (level)
  the two profiles are of different devices: /device:TPU:81 before, /device:TPU:88 now
where the time goes in v1:
time: 136 us
  Pallas kernels  133 us (98%)
  between operations  1.43 us (1%)
    pallas_call x2, Pallas kernels, exchange(): pl.pallas_call(functools.partial(comm_kernel, first), out_shape=out_shape...  36.8 us
    pallas_call x1, Pallas kernels, general(): pl.pallas_call(second_kernel, out_shape=shapes((4, 32, 128), (2, 32, 256)...  36.6 us
    pallas_call x1, Pallas kernels, fused(): pl.pallas_call(fused_kernel, out_shape=[jax.ShapeDtypeStruct((4, 32, 128)...  33.4 us
    pallas_call x1, Pallas kernels, general(): pl.pallas_call(first_kernel, out_shape=shapes((8, 32, 128), (8, 32, 128),...  25 us

profile of v1, /device:TPU:88, one launch (start us, length us, event | category | flops | bytes accessed | tf_op | source)
XLA Modules:
  0.0 136.0 jit_solution(14983727440188154320)
XLA Ops:
  0.6 0.0 copy-start
  0.6 0.0 copy-start.1
  0.7 0.0 copy-start.2
  0.7 0.0 copy-start.3
  0.7 0.0 copy-start.4
  0.7 0.0 copy-start.6
  0.7 0.0 copy-start.7
  0.7 33.4 %interval.1 = (f32[4,32,128]{2,1,0:T(8,128)S(1)}, f32[2,32,256]{2,1,0:T(8,128)S(1)}, f32[1,1]{1,0:T(1,128)}, s32[9,2,16]{2,1,0:T(2,128)S(1)}, s32[2,16]{1,0:T(2,128)S(1)}) custom-call(f32[2,32,256]{2,1,0:T(8,128)} %refs_0_.1, f32[32,256]{1,0:T(8,128)} %refs_1_.1, f32[2,32,128]{2,1,0:T(8,128)} %bitcast.16, f32[2,32,128]{2,1,0:T(8,128)} %bitcast.18, ...), custom_call_target="tpu_custom_call" | custom-call | tf_op jit(solution)/shard_map/interval/pallas_call | solution.py:1185
  34.2 0.0 copy-start.5
  34.8 0.0 copy-done
  34.8 0.0 copy-done.1
  34.8 0.0 copy-done.2
  34.8 0.0 copy-done.3
  34.9 0.0 copy-done.4
  34.9 0.0 copy-done.6
  34.9 0.0 copy-done.7
  34.9 0.0 copy-done.5
  34.9 99.9 %conditional.1 = ((f32[2,32,256]{2,1,0:T(8,128)S(1)}, f32[4,32,128]{2,1,0:T(8,128)S(1)})) conditional(s32[]{:T(128)} %bitcast.10, (f32[2,32,256]{2,1,0:T(8,128)S(1)}, f32[4,32,128]{2,1,0:T(8,128)S(1)}) %tuple.20, (f32[2,32,256]{2,1,0:T(8,128)S(1)}, f32[32,256]{1,0:T(8,128)S(1)}, f32[2,32,128]{2,1,0:T(8,128)S(1)}, f32[2,32,128]{2,1,0:T(8,128)S(1)}, ...), branch_computations={%region_0.0_spmd, %region_1.0_spmd} | conditional | bytes 24 | solution.py:1221
  34.9 1.5 %prepare.1 = (f32[8,32,128]{2,1,0:T(8,128)}, f32[8,32,128]{2,1,0:T(8,128)}, f32[8,128]{1,0:T(8,128)}) custom-call(f32[2,32,256]{2,1,0:T(8,128)S(1)} %get-tuple-element.31.gas.refs_3_, f32[32,256]{1,0:T(8,128)S(1)} %get-tuple-element.32.visc, f32[2,32,128]{2,1,0:T(8,128)S(1)} %get-tuple-element.33.pos, f32[2,32,128]{2,1,0:T(8,128)S(1)} %get-tuple-element.34.vel, ...), custom_call_target="tpu_custom_call" | custom-call | tf_op jit(solution)/shard_map/cond/branch_1_fun/prepare/pallas_call | solution.py:589
  36.4 17.8 %exchange_first.1 = (f32[8,128,128]{2,1,0:T(8,128)}, f32[8,32,128]{2,1,0:T(8,128)}, f32[8,128]{1,0:T(8,128)}, f32[2,2,8,256]{3,2,1,0:T(8,128)}, f32[2,2,32,128]{3,2,1,0:T(8,128)}) custom-call(f32[8,32,128]{2,1,0:T(8,128)} %get-tuple-element.37.refs_0_, f32[8,32,128]{2,1,0:T(8,128)} %get-tuple-element.38.refs_1_, f32[8,128]{1,0:T(8,128)} %get-tuple-element.39.refs_2_, ...), custom_call_target="tpu_custom_call" | custom-call | tf_op jit(solution)/shard_map/cond/branch_1_fun/exchange_first/pallas_call | solution.py:315
  54.2 25.0 %first_substep.1 = (f32[8,32,128]{2,1,0:T(8,128)}, f32[8,32,128]{2,1,0:T(8,128)}, f32[8,128]{1,0:T(8,128)}, f32[2,32,128]{2,1,0:T(8,128)}, f32[32,128]{1,0:T(8,128)}) custom-call(f32[1024,128]{1,0:T(8,128)} %bitcast.13, f32[8,32,128]{2,1,0:T(8,128)} %get-tuple-element.41.gv, f32[8,128]{1,0:T(8,128)} %get-tuple-element.42.rate, ...), custom_call_target="tpu_custom_call" | custom-call | tf_op jit(solution)/shard_map/cond/branch_1_fun/first_substep/pallas_call | solution.py:597
  79.2 19.0 %exchange_second.1 = (f32[8,128,128]{2,1,0:T(8,128)}, f32[8,32,128]{2,1,0:T(8,128)}, f32[8,128]{1,0:T(8,128)}) custom-call(f32[8,32,128]{2,1,0:T(8,128)} %get-tuple-element.47.refs_0_, f32[8,32,128]{2,1,0:T(8,128)} %get-tuple-element.48.refs_1_, f32[8,128]{1,0:T(8,128)} %get-tuple-element.49.refs_2_), custom_call_target="tpu_custom_call" | custom-call | tf_op jit(solution)/shard_map/cond/branch_1_fun/exchange_second/pallas_call | solution.py:315
  98.2 36.6 %second_substep.1 = (f32[4,32,128]{2,1,0:T(8,128)S(1)}, f32[2,32,256]{2,1,0:T(8,128)S(1)}) custom-call(f32[1024,128]{1,0:T(8,128)} %bitcast.12, f32[8,32,128]{2,1,0:T(8,128)} %get-tuple-element.51.dv, f32[8,128]{1,0:T(8,128)} %get-tuple-element.52.tot, f32[8,128]{1,0:T(8,128)} %get-tuple-element.42.rate, f32[2,32,128]{2,1,0:T(8,128)} %get-tuple-element.53.dr2, ...), custom_call_target="tpu_custom_call" | custom-call | tf_op jit(solution)/shard_map/cond/branch_1_fun/second_substep/pallas_call | solution.py:606
  134.8 0.6 copy.18
  135.4 0.6 copy.19
Async XLA Ops:
  0.6 34.2 %copy-start = (f32[2,32,256]{2,1,0:T(8,128)S(1)}, f32[2,32,256]{2,1,0:T(8,128)}, u32[]{:S(2)}) copy-start(f32[2,32,256]{2,1,0:T(8,128)} %refs_0_.1) | copy-start | bytes 196612
  0.6 34.2 %copy-start.1 = (f32[32,256]{1,0:T(8,128)S(1)}, f32[32,256]{1,0:T(8,128)}, u32[]{:S(2)}) copy-start(f32[32,256]{1,0:T(8,128)} %refs_1_.1) | copy-start | bytes 98308
  0.7 34.2 %copy-start.2 = (s32[2,16,2,128]{3,2,1,0:T(2,128)S(1)}, s32[2,16,2,128]{3,2,1,0:T(2,128)}, u32[]{:S(2)}) copy-start(s32[2,16,2,128]{3,2,1,0:T(2,128)} %param.21) | copy-start | bytes 98308
  0.7 34.2 %copy-start.3 = (f32[2,16,2,128]{3,2,1,0:T(2,128)S(1)}, f32[2,16,2,128]{3,2,1,0:T(2,128)}, u32[]{:S(2)}) copy-start(f32[2,16,2,128]{3,2,1,0:T(2,128)} %param.14) | copy-start | bytes 98308
  0.7 34.2 %copy-start.4 = (f32[2,16,2,128]{3,2,1,0:T(2,128)S(1)}, f32[2,16,2,128]{3,2,1,0:T(2,128)}, u32[]{:S(2)}) copy-start(f32[2,16,2,128]{3,2,1,0:T(2,128)} %param.15) | copy-start | bytes 98308
  0.7 34.2 %copy-start.6 = (s32[16,2,128]{2,1,0:T(2,128)S(1)}, s32[16,2,128]{2,1,0:T(2,128)}, u32[]{:S(2)}) copy-start(s32[16,2,128]{2,1,0:T(2,128)} %param.20) | copy-start | bytes 49156
  0.7 34.2 %copy-start.7 = (f32[16,2,128]{2,1,0:T(2,128)S(1)}, f32[16,2,128]{2,1,0:T(2,128)}, u32[]{:S(2)}) copy-start(f32[16,2,128]{2,1,0:T(2,128)} %param.16) | copy-start | bytes 49156
  34.2 0.7 copy-start.5
